TPU v7x, 512 devices: a whole 4x8x8 slice. The times are simulated.
512 devices in a mesh: len: 2 (over core), wid: 256 (over z, y, x).
Axes of the slice: x: 4, y: 8, z: 8, core: 2. Of those that a mesh axis runs over, the one named last changes fastest.
Arguments:
- latent: bfloat16 [4, 512, 128, 128], P('len', 'wid'), may hold values from -6 to 6
- offset: bfloat16 [4, 512, 3, 128], P('len', 'wid'), may hold values from 0 to 1
- occupied: int32 [4, 512, 128], P('len', 'wid'), may hold values 0 or 1
- pair_list: int32 [2, 256, 36], P('len', 'wid'), may hold values from -1 to 35, as said below
- w_send: bfloat16 [2, 128, 128], replicated, may hold values from -0.5 to 0.5
- w_recv: bfloat16 [2, 128, 128], replicated, may hold values from -0.5 to 0.5
- b_edge: float32 [2, 128], replicated, may hold values from -3 to 3
- w_disp: float32 [2, 3, 128], replicated, may hold values from -6 to 6
- w_dist: float32 [2, 128], replicated, may hold values from -6 to 6
- w_self: bfloat16 [2, 128, 128], replicated, may hold values from -0.5 to 0.5
- w_msg: bfloat16 [2, 128, 128], replicated, may hold values from -0.5 to 0.5
- b_node: float32 [2, 128], replicated, may hold values from -3 to 3
- w_out: bfloat16 [2, 128, 128], replicated, may hold values from -0.5 to 0.5
- gain: float32 [2, 128], replicated, may hold values from 0.5 to 1.5
Outputs:
- latent_out: bfloat16 [4, 512, 128, 128], P('len', 'wid')
Inputs may be any that keep to these rules, and one draw needn't show every extreme that they name: `pair_list`: entry list of each device: distinct codes c * 9 + d with c < 4 and d < 9, all before the first -1, the rest -1. A device at an even index across the slope lists 36 or 18 codes; one at an odd index lists 36 // 4 or 4 codes (at least 1); device (0, 0) lists all 36.
All inputs are finite; a program needn't handle non-finite values. No bound on the sum of `occupied` on one device may be relied on, other than what follows from the above.
Results may differ from a plain program's by a relative error of at most 0.0023.
The roundings to bfloat16 on the way count: a program that leaves them out, or rounds other values in their place, can miss the bound.
Values may be sent and summed in bfloat16 or wider, within the bound.
A program may use at most 64 MiB of HBM per device.

v0:
```python
import functools

import jax
import jax.numpy as jnp
from jax import lax
from jax.experimental import pallas as pl
from jax.experimental.pallas import tpu as pltpu
from jax.sharding import PartitionSpec as P

EPSILON = 1e-05
FAR = 64.0
F32 = jnp.float32
BF16 = jnp.bfloat16
ROWS = 144
VMEM = pl.BlockSpec(memory_space=pltpu.VMEM)
SMEM = pl.BlockSpec(memory_space=pltpu.SMEM)


def iota(shape, dim):
    return lax.broadcasted_iota(jnp.int32, shape, dim)


def swap_lanes(x, step):
    if step == 64:
        return pltpu.roll(x, 64, 1)
    low = (iota(x.shape, 1) & step) == 0
    return jnp.where(low, pltpu.roll(x, 128 - step, 1), pltpu.roll(x, step, 1))


def pick_lanes(x, index):
    return jnp.take_along_axis(x, index, axis=1)


def split_row(row):
    index = 16 * iota((8, 128), 0) + (iota((8, 128), 1) & 15)
    return pick_lanes(jnp.broadcast_to(row, (8, 128)), index)


def split_rows(src, dst):
    lane = iota((8, 128), 1)
    for base in range(0, src.shape[0], 64):
        parts = [src[pl.ds(base + m, 8, stride=8), :] for m in range(8)]
        for bit in (4, 2, 1):
            step = 16 * bit
            low = (lane & step) == 0
            for m in range(8):
                if m & bit:
                    continue
                a, b = parts[m], parts[m + bit]
                parts[m] = jnp.where(low, a, pltpu.roll(b, step, 1))
                parts[m + bit] = jnp.where(low, pltpu.roll(a, 128 - step, 1), b)
        for q in range(8):
            dst[pl.ds(base + q, 8, stride=8), :] = parts[q]


def project(state, step, w_send, w_recv, b_edge, w_disp, place, msg, recv, flat, split):
    flat[...] = jnp.dot(state, w_send[step], preferred_element_type=F32)
    split_rows(flat, split)
    r = jnp.dot(state, w_recv[step], preferred_element_type=F32) + b_edge[step : step + 1, :]
    r = r.astype(BF16).astype(F32)
    for cell in range(4):
        here = slice(cell * 128, cell * 128 + 128)
        msg[cell, 0:128, :] = split[here, :].astype(BF16)
        pull = sum(place[cell, k] * w_disp[step, k : k + 1, :] for k in range(3))
        recv[cell] = r[here] - pull


def prepare(latent, offset, occupied, w_send, w_recv, b_edge, w_disp, state, ranks, msg, recv, place, flat, split):
    upper = (iota((128, 128), 0) < iota((128, 128), 1)).astype(F32).astype(BF16)
    occ = occupied[...].astype(F32)
    before = jnp.dot(occ.astype(BF16), upper, preferred_element_type=F32)
    total = jnp.sum(occ, axis=1, keepdims=True)
    lane = iota((4, 128), 1).astype(F32)
    rank = jnp.where(occ > 0.5, before, total + lane - before)
    ranks[...] = rank
    slot = iota((128, 128), 0).astype(F32)
    for row in range(2):
        for col in range(2):
            given, cell = row * 2 + col, col * 2 + row
            perm = (slot == rank[given : given + 1, :]).astype(F32).astype(BF16)
            ordered = jnp.dot(perm, latent[given], preferred_element_type=F32).astype(BF16)
            state[cell] = ordered
            held = iota((128, 128), 0).astype(F32) < total[given : given + 1, :]
            for k in range(3):
                line = jnp.broadcast_to(offset[given, k : k + 1, :].astype(F32), (128, 128)).astype(BF16)
                spread = lax.dot_general(perm, line, (((1,), (1,)), ((), ())), preferred_element_type=F32)
                place[cell, k] = jnp.where(held, spread, -FAR) if k == 2 else spread
            geo = jnp.concatenate(
                [offset[given].astype(F32), occ[given : given + 1], jnp.zeros((12, 128), F32)], axis=0
            ).astype(BF16)
            moved = lax.dot_general(geo, perm, (((1,), (1,)), ((), ())), preferred_element_type=F32)
            msg[cell, 128:ROWS, :] = moved.astype(BF16)
    project(state[...].reshape(512, 128), 0, w_send, w_recv, b_edge, w_disp, place, msg, recv, flat, split)


def exchange(msg, grid, send_sem, recv_sem, own_sem):
    me_len, me_wid = lax.axis_index("len"), lax.axis_index("wid")
    count = lax.axis_size("wid")
    right, left = lax.rem(me_wid + 1, count), lax.rem(me_wid + count - 1, count)
    other = 1 - me_len
    barrier = pltpu.get_barrier_semaphore()
    for peer in ((me_len, left), (me_len, right), (other, me_wid), (other, left), (other, right)):
        pl.semaphore_signal(barrier, inc=1, device_id=peer, device_id_type=pl.DeviceIdType.MESH)
    own = pltpu.make_async_copy(msg, grid.at[pl.ds(0, 4)], own_sem)
    own.start()
    pl.semaphore_wait(barrier, 5)
    edge = 1 - me_len
    plan = (
        (pl.ds(0, 2), pl.ds(6, 2), (me_len, left)),
        (pl.ds(2, 2), pl.ds(4, 2), (me_len, right)),
        (pl.ds(edge, 1), pl.ds(11, 1), (other, left)),
        (pl.ds(2 + edge, 1), pl.ds(8, 1), (other, right)),
        (pl.ds(edge, 1), pl.ds(9, 1), (other, me_wid)),
        (pl.ds(2 + edge, 1), pl.ds(10, 1), (other, me_wid)),
    )
    copies = []
    for k, (src, dst, peer) in enumerate(plan):
        copy = pltpu.make_async_remote_copy(
            src_ref=msg.at[src],
            dst_ref=grid.at[dst],
            send_sem=send_sem.at[k],
            recv_sem=recv_sem.at[k],
            device_id=peer,
            device_id_type=pl.DeviceIdType.MESH,
        )
        copy.start()
        copies.append(copy)
    for copy in copies:
        copy.wait()
    own.wait()


def pairs(step, last, *refs):
    codes, grid, recv, place, state, ranks, w_send, w_recv, b_edge, w_disp, w_dist = refs[:11]
    w_self, w_msg, b_node, w_out, gain = refs[11:16]
    if last:
        (out,) = refs[16:17]
        rest = refs[17:]
    else:
        state_out, msg, recv_out = refs[16:19]
        rest = refs[19:]
    acc, floor, csum, sent, spots, far, close, counts, incoming, flat, split = rest
    me_len = lax.axis_index("len")

    for cell in range(12):
        geo = grid[cell, 128:ROWS, :].astype(F32)
        for k in range(3):
            row = geo[k : k + 1]
            if k == 2:
                row = row + FAR * (1.0 - geo[3:4])
            row = jnp.broadcast_to(row, (8, 128))
            index = 8 * iota((8, 128), 0) + (iota((8, 128), 1) >> 4)
            spots[cell, k, 0:8, :] = pick_lanes(row, index)
            spots[cell, k, 8:16, :] = pick_lanes(row, index + 64)
        counts[cell] = jnp.sum(geo[3:4]).astype(jnp.int32)

    acc[...] = jnp.zeros_like(acc)
    csum[...] = jnp.zeros_like(csum)
    incoming[...] = jnp.zeros_like(incoming)

    for cell in range(4):

        def spread_recv(group, _, cell=cell):
            for t in range(4):
                at = pl.multiple_of(group * 32 + 8 * t, 8)
                x = -recv[cell, pl.ds(at, 8), :]
                for q in range(8):
                    part = pick_lanes(x, 16 * q + (iota((8, 128), 1) & 15))
                    floor[pl.ds((cell * 128 + at) * 8 + q, 8, stride=8), :] = part
            return 0

        lax.fori_loop(0, (counts[cell] + 31) >> 5, spread_recv, 0)

    push = [split_row(w_disp[step, k : k + 1, :]) for k in range(3)]
    pull = split_row(w_dist[step : step + 1, :])

    def one_pair(p, _):
        code = codes[p]
        given = (code * 57) >> 9
        direction = code - given * 9
        row, col = given >> 1, given & 1
        high = (direction * 11) >> 5
        up, side = high - 1, direction - high * 3 - 1
        cell = col * 2 + row
        at_row, at_col = row + 1 + up, col + 1 + side
        in_rows = (at_row == 1) | (at_row == 2)
        in_cols = (at_col == 1) | (at_col == 2)
        beyond = at_row == jnp.where(me_len == 0, 3, 0)
        source = jnp.where(
            in_rows & in_cols,
            (at_col - 1) * 2 + at_row - 1,
            jnp.where(in_rows, jnp.where(at_col == 3, 6, 4) + at_row - 1, 8 + at_col),
        )

        @pl.when(in_rows | beyond)
        def _():
            here, there = counts[cell], counts[source]
            shift = [jnp.full((1, 128), s.astype(F32)) for s in (up, side)]
            lines = (there + 7) >> 3

            def fill(b, _):
                for r in range(4):
                    at = b * 4 + r
                    rows = pl.ds(pl.multiple_of(at * 8, 8), 8)
                    ox = spots[source, 0, pl.ds(at, 1), :] + shift[0]
                    oy = spots[source, 1, pl.ds(at, 1), :] + shift[1]
                    oz = spots[source, 2, pl.ds(at, 1), :]
                    s = grid[source, rows, :].astype(F32)
                    sent[rows, :] = s + ox * push[0] + oy * push[1] + oz * push[2]
                return 0

            lax.fori_loop(0, (lines + 3) >> 2, fill, 0)

            def block_of(tiles, tile, _):
                many = 8 * tiles
                start = pl.multiple_of(cell * 128 + tile * 8, 8)
                rows = [pl.ds(pl.multiple_of(tile * 8 + 8 * t, 8), 8) for t in range(tiles)]
                ox = [place[cell, 0, rows[t], :] - shift[0] for t in range(tiles)]
                oy = [place[cell, 1, rows[t], :] - shift[1] for t in range(tiles)]
                oz = [place[cell, 2, rows[t], :] for t in range(tiles)]

                def measure(b, weight):
                    weight = list(weight)
                    for r in range(4):
                        at = b * 4 + r
                        x = spots[source, 0, pl.ds(at, 1), :]
                        y = spots[source, 1, pl.ds(at, 1), :]
                        z = spots[source, 2, pl.ds(at, 1), :]
                        for t in range(tiles):
                            dx, dy, dz = ox[t] - x, oy[t] - y, oz[t] - z
                            d = dx * dx + dy * dy + dz * dz
                            c = jnp.maximum(1.0 - d, 0.0)
                            c = c * c
                            put = pl.ds(pl.multiple_of(at * 16 + 8 * t, 8), 8)
                            far[put, :] = d
                            close[put, :] = c
                            weight[t] = weight[t] + c
                    return tuple(weight)

                weight = tuple(csum[pl.ds(start + 8 * t, 8), :] for t in range(tiles))
                weight = lax.fori_loop(0, (lines + 3) >> 2, measure, weight)
                for t in range(tiles):
                    csum[pl.ds(start + 8 * t, 8), :] = weight[t]

                first = pl.multiple_of(start * 8, 64)
                nr = [floor[pl.ds(first + 8 * i, 8), :] for i in range(many)]

                def senders(width, at, carry):
                    total = list(carry)
                    for r in range(width):
                        s = sent[pl.ds(pl.multiple_of((at + r) * 8, 8), 8), :]
                        for i in range(many):
                            d = far[pl.ds((at + r) * 16 + i, 1), :]
                            c = close[pl.ds((at + r) * 16 + i, 1), :]
                            total[i] = total[i] + c * jnp.maximum(s + d * pull, nr[i])
                    return tuple(total)

                total = tuple(acc[pl.ds(first + 8 * i, 8), :] for i in range(many))
                total = lax.fori_loop(0, lines >> 1, lambda b, c: senders(2, 2 * b, c), total)
                total = lax.fori_loop(lines & ~1, lines, lambda b, c: senders(1, b, c), total)
                for i in range(many):
                    acc[pl.ds(first + 8 * i, 8), :] = total[i]
                return 0

            wide = (here + 7) >> 3
            lax.fori_loop(0, wide >> 1, lambda b, c: block_of(2, 2 * b, c), 0)
            lax.fori_loop(wide & ~1, wide, lambda b, c: block_of(1, b, c), 0)

        return 0

    listed = sum((codes[p] >= 0).astype(jnp.int32) for p in range(codes.shape[0]))
    lax.fori_loop(0, listed, one_pair, 0)

    for cell in range(4):

        def gather(group, _, cell=cell):
            lane = iota((8, 128), 1)
            for t in range(4):
                at = pl.multiple_of(group * 32 + 8 * t, 8)
                base = (cell * 128 + at) * 8
                parts = [acc[pl.ds(base + q, 8, stride=8), :] for q in range(8)]
                for bit in (4, 2, 1):
                    low = (lane & (16 * bit)) == 0
                    parts = [
                        jnp.where(low, parts[q], parts[q + bit])
                        + swap_lanes(jnp.where(low, parts[q + bit], parts[q]), 16 * bit)
                        for q in range(bit)
                    ]
                weight = jnp.sum(csum[pl.ds(cell * 128 + at, 8), :], axis=1, keepdims=True) * (1.0 / 16.0)
                incoming[pl.ds(cell * 128 + at, 8), :] = parts[0] + recv[cell, pl.ds(at, 8), :] * weight
            return 0

        lax.fori_loop(0, (counts[cell] + 31) >> 5, gather, 0)

    h = state[...].reshape(512, 128)
    msg_in = (incoming[...] * (8.0 / 128.0)).astype(BF16)
    pre = (
        jnp.dot(h, w_self[step], preferred_element_type=F32)
        + jnp.dot(msg_in, w_msg[step], preferred_element_type=F32)
        + b_node[step : step + 1, :]
    )
    hidden = jnp.maximum(pre, 0.0).astype(BF16)
    y = jnp.dot(hidden, w_out[step], preferred_element_type=F32)
    center = jnp.mean(y, axis=-1, keepdims=True)
    spread = jnp.mean(jnp.square(y - center), axis=-1, keepdims=True)
    normed = (y - center) / jnp.sqrt(spread + EPSILON)
    new = (h.astype(F32) + normed * gain[step : step + 1, :]).astype(BF16)
    if last:
        slot = iota((128, 128), 0).astype(F32)
        for cell in range(4):
            given = (cell & 1) * 2 + (cell >> 1)
            perm = (slot == ranks[given : given + 1, :]).astype(F32).astype(BF16)
            here = new[cell * 128 : cell * 128 + 128]
            back = lax.dot_general(perm, here, (((0,), (0,)), ((), ())), preferred_element_type=F32)
            out[given] = back.astype(BF16)
    else:
        state_out[...] = new.reshape(4, 128, 128)
        for cell in range(4):
            msg[cell, 128:ROWS, :] = grid[cell, 128:ROWS, :]
        project(new, 1, w_send, w_recv, b_edge, w_disp, place, msg, recv_out, flat, split)


def per_device(
    latent, offset, occupied, pair_list, w_send, w_recv, b_edge, w_disp, w_dist, w_self, w_msg, b_node, w_out, gain
):
    shape = jax.ShapeDtypeStruct
    state, ranks, msg, recv, place = pl.pallas_call(
        prepare,
        name="prepare",
        out_shape=(
            shape((4, 128, 128), BF16),
            shape((4, 128), F32),
            shape((4, ROWS, 128), BF16),
            shape((4, 128, 128), F32),
            shape((4, 3, 128, 128), F32),
        ),
        in_specs=[VMEM] * 7,
        out_specs=(VMEM,) * 5,
        scratch_shapes=[pltpu.VMEM((512, 128), F32)] * 2,
    )(
        latent.reshape(4, 128, 128),
        offset.reshape(4, 3, 128),
        occupied.reshape(4, 128),
        w_send,
        w_recv,
        b_edge,
        w_disp,
    )
    swap = pl.pallas_call(
        exchange,
        name="exchange",
        out_shape=shape((12, ROWS, 128), BF16),
        in_specs=[VMEM],
        out_specs=VMEM,
        scratch_shapes=[pltpu.SemaphoreType.DMA((6,)), pltpu.SemaphoreType.DMA((6,)), pltpu.SemaphoreType.DMA],
        compiler_params=pltpu.CompilerParams(collective_id=0, has_side_effects=True),
    )
    codes = pair_list.reshape(-1)
    for step in range(2):
        last = step == 1
        grid = swap(msg)
        if last:
            out_shape = shape((4, 128, 128), BF16)
            out_specs = VMEM
        else:
            out_shape = (shape((4, 128, 128), BF16), shape((4, ROWS, 128), BF16), shape((4, 128, 128), F32))
            out_specs = (VMEM,) * 3
        made = pl.pallas_call(
            functools.partial(pairs, step, last),
            name=f"pairs_{step}",
            out_shape=out_shape,
            in_specs=[SMEM] + [VMEM] * 15,
            out_specs=out_specs,
            scratch_shapes=[
                pltpu.VMEM((4096, 128), F32),
                pltpu.VMEM((4096, 128), F32),
                pltpu.VMEM((512, 128), F32),
                pltpu.VMEM((128, 128), F32),
                pltpu.VMEM((12, 3, 16, 128), F32),
                pltpu.VMEM((256, 128), F32),
                pltpu.VMEM((256, 128), F32),
                pltpu.SMEM((12,), jnp.int32),
                pltpu.VMEM((512, 128), F32),
                pltpu.VMEM((512, 128), F32),
                pltpu.VMEM((512, 128), F32),
            ],
        )(
            codes, grid, recv, place, state, ranks, w_send, w_recv, b_edge, w_disp, w_dist, w_self, w_msg, b_node,
            w_out, gain,
        )
        if not last:
            state, msg, recv = made
    return made.reshape(latent.shape)


def solution(mesh):
    return jax.shard_map(
        per_device,
        mesh=mesh,
        in_specs=(
            P("len", "wid", None, None),
            P("len", "wid", None, None),
            P("len", "wid", None),
            P("len", "wid", None),
        )
        + (P(),) * 10,
        out_specs=P("len", "wid", None, None),
        check_vma=False,
    )
```

profile of v0, /device:TPU:257, one launch (start us, length us, event | category | flops | bytes accessed | tf_op | source)
XLA Modules:
  0.0 106.4 jit_solution(5589741793205232114)
XLA Ops:
  0.0 0.0 copy-start
  0.0 0.7 copy-done
  0.7 0.0 copy-start.1
  0.7 0.6 copy.16.w_disp.refs_9_
  1.3 0.1 copy-done.1
  1.4 0.6 copy.15
  2.0 2.7 %prepare.1 = (bf16[4,128,128]{2,1,0:T(8,128)(2,1)}, f32[4,128]{1,0:T(4,128)}, bf16[4,144,128]{2,1,0:T(8,128)(2,1)}, f32[4,128,128]{2,1,0:T(8,128)}, f32[4,3,128,128]{3,2,1,0:T(8,128)}) custom-call(bf16[4,128,128]{2,1,0:T(8,128)(2,1)} %bitcast.5, bf16[4,3,128]{2,1,0:T(4,128)(2,1)} %bitcast.6, s32[4,128]{1,0:T(4,128)} %bitcast.7, ...), custom_call_target="tpu_custom_call" | custom-call | tf_op jit(solution)/shard_map/prepare/pallas_call | solution.py:327
  4.7 13.3 %exchange.2.refs_1_ = bf16[12,144,128]{2,1,0:T(8,128)(2,1)} custom-call(bf16[4,144,128]{2,1,0:T(8,128)(2,1)} %get-tuple-element.13.msg), custom_call_target="tpu_custom_call" | custom-call | tf_op jit(solution)/shard_map/exchange/pallas_call | solution.py:361
  18.0 38.0 %pairs_0.1 = (bf16[4,128,128]{2,1,0:T(8,128)(2,1)}, bf16[4,144,128]{2,1,0:T(8,128)(2,1)}, f32[4,128,128]{2,1,0:T(8,128)}) custom-call(s32[36]{0:T(128)} %bitcast.8, bf16[12,144,128]{2,1,0:T(8,128)(2,1)} %exchange.2.refs_1_, f32[4,128,128]{2,1,0:T(8,128)} %get-tuple-element.14.refs_2_, f32[4,3,128,128]{3,2,1,0:T(8,128)} %get-tuple-element.15.refs_3_, ...), custom_call_target="tpu_custom_call" | custom-call | tf_op jit(solution)/shard_map/pairs_0/pallas_call | solution.py:368
  56.0 12.7 %exchange.3.refs_1_ = bf16[12,144,128]{2,1,0:T(8,128)(2,1)} custom-call(bf16[4,144,128]{2,1,0:T(8,128)(2,1)} %get-tuple-element.18.msg), custom_call_target="tpu_custom_call" | custom-call | tf_op jit(solution)/shard_map/exchange/pallas_call | solution.py:361
  68.7 37.7 %pairs_1.1 = bf16[4,128,128]{2,1,0:T(8,128)(2,1)} custom-call(s32[36]{0:T(128)} %bitcast.9, bf16[12,144,128]{2,1,0:T(8,128)(2,1)} %exchange.3.refs_1_, f32[4,128,128]{2,1,0:T(8,128)} %get-tuple-element.19.refs_2_, f32[4,3,128,128]{3,2,1,0:T(8,128)} %get-tuple-element.15.refs_3_, bf16[4,128,128]{2,1,0:T(8,128)(2,1)} %get-tuple-element.20.refs_4_, ...), custom_call_target="tpu_custom_call" | custom-call | tf_op jit(solution)/shard_map/pairs_1/pallas_call | solution.py:368
Async XLA Ops:
  0.0 0.7 copy-start
  0.7 0.7 copy-start.1
where the time goes:
time: 108 us; the launch traced here: 106 us
  Pallas kernels  104 us (96%)
  local copies, waits for them, and re-layouts  1.96 us (2%)
    pallas_call x2, Pallas kernels, per_device(): pl.pallas_call(functools.partial(pairs, step, last), name=f'pairs_{step}'...  75.7 us
    pallas_call x2, Pallas kernels, per_device(): grid = swap(msg)  26 us
    pallas_call x1, Pallas kernels, per_device(): pl.pallas_call(prepare, name='prepare', out_shape=(shape((4, 128, 128), B...  2.72 us

commit v1 on v0

v1 whole, which is shorter than its diff:
```python
import functools

import jax
import jax.numpy as jnp
from jax import lax
from jax.experimental import pallas as pl
from jax.experimental.pallas import tpu as pltpu
from jax.sharding import PartitionSpec as P

EPSILON = 1e-05
FAR = 64.0
F32 = jnp.float32
BF16 = jnp.bfloat16
ROWS = 144
LIMIT = 16 << 20
VMEM = pl.BlockSpec(memory_space=pltpu.VMEM)
FIXED = pl.BlockSpec(memory_space=pltpu.HBM)
SMEM = pl.BlockSpec(memory_space=pltpu.SMEM)


def iota(shape, dim):
    return lax.broadcasted_iota(jnp.int32, shape, dim)


def swap_lanes(x, step):
    if step == 64:
        return pltpu.roll(x, 64, 1)
    low = (iota(x.shape, 1) & step) == 0
    return jnp.where(low, pltpu.roll(x, 128 - step, 1), pltpu.roll(x, step, 1))


def pick_lanes(x, index):
    return jnp.take_along_axis(x, index, axis=1)


def split_row(row):
    index = 16 * iota((8, 128), 0) + (iota((8, 128), 1) & 15)
    return pick_lanes(jnp.broadcast_to(row, (8, 128)), index)


def split_rows(src, dst):
    lane = iota((8, 128), 1)
    for base in range(0, src.shape[0], 64):
        parts = [src[pl.ds(base + m, 8, stride=8), :] for m in range(8)]
        for bit in (4, 2, 1):
            step = 16 * bit
            low = (lane & step) == 0
            for m in range(8):
                if m & bit:
                    continue
                a, b = parts[m], parts[m + bit]
                parts[m] = jnp.where(low, a, pltpu.roll(b, step, 1))
                parts[m + bit] = jnp.where(low, pltpu.roll(a, 128 - step, 1), b)
        for q in range(8):
            dst[pl.ds(base + q, 8, stride=8), :] = parts[q]


def project_send(state, step, w_send, msg, flat, split):
    flat[...] = jnp.dot(state, w_send[step], preferred_element_type=F32)
    split_rows(flat, split)
    for cell in range(4):
        msg[cell, 0:128, :] = split[cell * 128 : cell * 128 + 128, :].astype(BF16)


def project_recv(state, step, w_recv, b_edge, w_disp, place, recv):
    r = jnp.dot(state, w_recv[step], preferred_element_type=F32) + b_edge[step : step + 1, :]
    r = r.astype(BF16).astype(F32)
    for cell in range(4):
        pull = sum(place[cell, k] * w_disp[k, step : step + 1, :] for k in range(3))
        recv[cell] = r[cell * 128 : cell * 128 + 128] - pull


def peers():
    me_len, me_wid = lax.axis_index("len"), lax.axis_index("wid")
    count = lax.axis_size("wid")
    right, left = lax.rem(me_wid + 1, count), lax.rem(me_wid + count - 1, count)
    return me_len, me_wid, left, right


def greet():
    me_len, me_wid, left, right = peers()
    other = 1 - me_len
    barrier = pltpu.get_barrier_semaphore()
    for peer in ((me_len, left), (me_len, right), (other, me_wid), (other, left), (other, right)):
        pl.semaphore_signal(barrier, inc=1, device_id=peer, device_id_type=pl.DeviceIdType.MESH)


def send_all(msg, grid, send_sem, recv_sem, own_sem):
    me_len, me_wid, left, right = peers()
    other = 1 - me_len
    edge = 1 - me_len
    pl.semaphore_wait(pltpu.get_barrier_semaphore(), 5)
    plan = (
        (pl.ds(0, 2), pl.ds(6, 2), (me_len, left)),
        (pl.ds(2, 2), pl.ds(4, 2), (me_len, right)),
        (pl.ds(edge, 1), pl.ds(11, 1), (other, left)),
        (pl.ds(2 + edge, 1), pl.ds(8, 1), (other, right)),
        (pl.ds(edge, 1), pl.ds(9, 1), (other, me_wid)),
        (pl.ds(2 + edge, 1), pl.ds(10, 1), (other, me_wid)),
    )
    copies = []
    for k, (src, dst, peer) in enumerate(plan):
        copy = pltpu.make_async_remote_copy(
            src_ref=msg.at[src],
            dst_ref=grid.at[dst],
            send_sem=send_sem.at[k],
            recv_sem=recv_sem.at[k],
            device_id=peer,
            device_id_type=pl.DeviceIdType.MESH,
        )
        copy.start()
        copies.append(copy)
    own = pltpu.make_async_copy(msg, grid.at[pl.ds(0, 4)], own_sem)
    own.start()
    return copies + [own]


def begin(latent_in, offset, occupied, w_send_in, w_recv_in, b_edge, w_disp, *refs):
    state, ranks, recv, place, grid, table, msg, flat, split, send_sem, recv_sem, own_sem = refs[:12]
    latent, w_send, w_recv, load_sem = refs[12:]
    greet()
    loads = [
        pltpu.make_async_copy(src, dst, load_sem.at[k])
        for k, (src, dst) in enumerate(((latent_in, latent), (w_send_in, w_send), (w_recv_in, w_recv)))
    ]
    for load in loads:
        load.start()
    occ = occupied[...].astype(F32)
    total = jnp.sum(occ, axis=1, keepdims=True)
    line, lane = iota((128, 128), 0), iota((128, 128), 1)
    slot = line.astype(F32)
    same = (line == lane).astype(F32).astype(BF16)
    both = (((1,), (1,)), ((), ()))
    perms = [None] * 4
    for row in range(2):
        for col in range(2):
            given, cell = row * 2 + col, col * 2 + row
            held = occ[given : given + 1]
            key = (offset[row, 1, col : col + 1, :].astype(F32) + 2.0 * (1.0 - held)).astype(BF16)
            key_row = jnp.broadcast_to(key.astype(F32), (128, 128))
            key_col = lax.dot_general(same, key_row.astype(BF16), both, preferred_element_type=F32)
            ahead = (key_col < key_row) | ((key_col == key_row) & (line < lane))
            rank = jnp.sum(ahead.astype(F32), axis=0, keepdims=True)
            ranks[given : given + 1, :] = rank
            perm = (slot == rank).astype(F32).astype(BF16)
            perms[cell] = perm
            full = slot < total[given : given + 1, :]
            for k in range(3):
                part = jnp.broadcast_to(offset[row, k, col : col + 1, :].astype(F32), (128, 128)).astype(BF16)
                spread = lax.dot_general(perm, part, both, preferred_element_type=F32)
                place[cell, k] = jnp.where(full, spread, -FAR) if k == 2 else spread
            geo = [offset[row, k, col : col + 1, :].astype(F32) for k in range(3)]
            geo = jnp.concatenate(geo + [held, jnp.zeros((12, 128), F32)], axis=0).astype(BF16)
            moved = lax.dot_general(geo, perm, both, preferred_element_type=F32)
            msg[cell, 128:ROWS, :] = moved.astype(BF16)
    for load in loads:
        load.wait()
    for cell in range(4):
        given = (cell & 1) * 2 + (cell >> 1)
        state[cell] = jnp.dot(perms[cell], latent[given], preferred_element_type=F32).astype(BF16)
    project_send(state[...].reshape(512, 128), 0, w_send, msg, flat, split)
    project_recv(state[...].reshape(512, 128), 0, w_recv, b_edge, w_disp, place, recv)
    for copy in send_all(msg, grid, send_sem, recv_sem, own_sem):
        copy.wait()
    wide_lane = iota((1, 128), 1)
    step = (wide_lane * 8) & 127
    tall = iota((16, 128), 0)
    table_lane = iota((64, 128), 1)
    tops, bottoms = [], []
    for cell in range(4):
        given = (cell & 1) * 2 + (cell >> 1)
        inside = (tall * 8 + 7).astype(F32) < total[given : given + 1, :]
        tops.append(jnp.where(inside, place[cell, 1, pl.ds(7, 16, stride=8), :], 2.0))
        bottoms.append(place[cell, 1, pl.ds(0, 16, stride=8), :])
    top, bottom = jnp.concatenate(tops, axis=0), jnp.concatenate(bottoms, axis=0)
    high, low = jnp.zeros((64, 128), F32), jnp.zeros((64, 128), F32)
    held = jnp.zeros((1, 128), F32)
    for cell in range(12):
        geo = grid[cell, 128:ROWS, :].astype(F32)
        count = jnp.sum(geo[3:4], axis=1, keepdims=True)
        mine = table_lane == cell
        held = jnp.where(wide_lane == cell, count, held)
        at = (wide_lane * 8).astype(F32)
        begins = pick_lanes(jnp.broadcast_to(geo[1:2], (8, 128)), jnp.broadcast_to(step, (8, 128)))[0:1]
        ends = pick_lanes(jnp.broadcast_to(geo[1:2], (8, 128)), jnp.broadcast_to(step + 7, (8, 128)))[0:1]
        begins = jnp.where(at < count, begins, 4.0)
        ends = jnp.where(at + 7.0 < count, ends, 4.0)
        high = jnp.where(mine, jnp.sum((begins < top).astype(F32), axis=1, keepdims=True), high)
        low = jnp.where(mine, jnp.sum((ends <= bottom).astype(F32), axis=1, keepdims=True), low)
    table[0:64, :] = high.astype(jnp.int32)
    table[64:128, :] = low.astype(jnp.int32)
    table[128:136, :] = jnp.broadcast_to(held, (8, 128)).astype(jnp.int32)


def node_update(step, state, msg_in, w_self, w_msg, b_node, w_out, gain):
    h = state[...].reshape(512, 128)
    pre = (
        jnp.dot(h, w_self[step], preferred_element_type=F32)
        + jnp.dot(msg_in, w_msg[step], preferred_element_type=F32)
        + b_node[step : step + 1, :]
    )
    hidden = jnp.maximum(pre, 0.0).astype(BF16)
    y = jnp.dot(hidden, w_out[step], preferred_element_type=F32)
    center = jnp.mean(y, axis=-1, keepdims=True)
    spread = jnp.mean(jnp.square(y - center), axis=-1, keepdims=True)
    normed = (y - center) / jnp.sqrt(spread + EPSILON)
    return (h.astype(F32) + normed * gain[step : step + 1, :]).astype(BF16)


def middle(state, msg_in, before, place, w_send, w_recv, b_edge, w_disp, *refs):
    w_self, w_msg, b_node, w_out, gain = refs[:5]
    state_out, recv, grid, msg, flat, split, send_sem, recv_sem, own_sem = refs[5:]
    greet()
    new = node_update(0, state, msg_in[...], w_self, w_msg, b_node, w_out, gain)
    state_out[...] = new.reshape(4, 128, 128)
    for cell in range(4):
        msg[cell, 128:ROWS, :] = before[cell, 128:ROWS, :]
    project_send(new, 1, w_send, msg, flat, split)
    project_recv(new, 1, w_recv, b_edge, w_disp, place, recv)
    for copy in send_all(msg, grid, send_sem, recv_sem, own_sem):
        copy.wait()


def pairs(step, last, codes, table, grid, recv, place, w_disp, w_dist, *refs):
    if last:
        state, ranks, w_self, w_msg, b_node, w_out, gain, out = refs[:8]
        rest = refs[8:]
    else:
        (msg_in,) = refs[:1]
        rest = refs[1:]
    acc, floor, csum, sent, queue, spots, far, close, incoming, plan, many = rest
    me_len = lax.axis_index("len")
    counts = [table[128, cell] for cell in range(4)]

    for cell in range(12):
        geo = grid[cell, 128:ROWS, :].astype(F32)
        for k in range(3):
            row = geo[k : k + 1]
            if k == 2:
                row = row + FAR * (1.0 - geo[3:4])
            row = jnp.broadcast_to(row, (8, 128))
            index = 8 * iota((8, 128), 0) + (iota((8, 128), 1) >> 4)
            spots[cell, k, 0:8, :] = pick_lanes(row, index)
            spots[cell, k, 8:16, :] = pick_lanes(row, index + 64)
            spots[cell, k, 16:24, :] = jnp.full((8, 128), FAR)

    acc[...] = jnp.zeros_like(acc)
    csum[...] = jnp.zeros_like(csum)
    incoming[...] = jnp.zeros_like(incoming)

    for cell in range(4):

        def spread_recv(group, _, cell=cell):
            for t in range(4):
                at = pl.multiple_of(group * 32 + 8 * t, 8)
                x = -recv[cell, pl.ds(at, 8), :]
                for q in range(8):
                    part = pick_lanes(x, 16 * q + (iota((8, 128), 1) & 15))
                    floor[pl.ds((cell * 128 + at) * 8 + q, 8, stride=8), :] = part
            return 0

        lax.fori_loop(0, (counts[cell] + 31) >> 5, spread_recv, 0)

    push = [split_row(w_disp[k, step : step + 1, :]) for k in range(3)]
    pull = split_row(w_dist[step : step + 1, :])

    for cell in range(4):
        many[cell] = 0

    def enlist(p, _):
        code = codes[p]
        given = (code * 57) >> 9
        direction = code - given * 9
        row, col = given >> 1, given & 1
        high = (direction * 11) >> 5
        up, side = high - 1, direction - high * 3 - 1
        cell = col * 2 + row
        at_row, at_col = row + 1 + up, col + 1 + side
        in_rows = (at_row == 1) | (at_row == 2)
        in_cols = (at_col == 1) | (at_col == 2)
        beyond = at_row == jnp.where(me_len == 0, 3, 0)
        source = jnp.where(
            in_rows & in_cols,
            (at_col - 1) * 2 + at_row - 1,
            jnp.where(in_rows, jnp.where(at_col == 3, 6, 4) + at_row - 1, 8 + at_col),
        )

        @pl.when(in_rows | beyond)
        def _():
            spot = many[cell]
            plan[cell, 3 * spot] = source
            plan[cell, 3 * spot + 1] = up
            plan[cell, 3 * spot + 2] = side
            many[cell] = spot + 1

        return 0

    listed = sum((codes[p] >= 0).astype(jnp.int32) for p in range(codes.shape[0]))
    lax.fori_loop(0, listed, enlist, 0)

    def one_cell(cell, _):
        here, entries = table[128, cell], many[cell]

        def fill(q, _):
            source, up, side = (plan[cell, 3 * q + k] for k in range(3))
            shift = [jnp.full((1, 128), s.astype(F32)) for s in (up, side)]

            def some(b, _):
                for r in range(4):
                    at = b * 4 + r
                    ox = spots[source, 0, pl.ds(at, 1), :] + shift[0]
                    oy = spots[source, 1, pl.ds(at, 1), :] + shift[1]
                    oz = spots[source, 2, pl.ds(at, 1), :]
                    s = grid[source, pl.ds(pl.multiple_of(at * 8, 8), 8), :].astype(F32)
                    put = pl.ds(pl.multiple_of(q * 160 + at * 8, 8), 8)
                    sent[put, :] = s + ox * push[0] + oy * push[1] + oz * push[2]
                return 0

            return lax.fori_loop(0, (table[128, source] + 31) >> 5, some, 0)

        lax.fori_loop(0, entries, fill, 0)

        def block_of(tiles, tile):
            size = 8 * tiles
            start = pl.multiple_of(cell * 128 + tile * 8, 8)
            rows = [pl.ds(pl.multiple_of(tile * 8 + 8 * t, 8), 8) for t in range(tiles)]
            place_x = [place[cell, 0, rows[t], :] for t in range(tiles)]
            place_y = [place[cell, 1, rows[t], :] for t in range(tiles)]
            oz = [place[cell, 2, rows[t], :] for t in range(tiles)]

            def measure(q, carry):
                front, weight = carry[0], carry[1:]
                source, up, side = (plan[cell, 3 * q + k] for k in range(3))
                lines = (table[128, source] + 7) >> 3
                most = jnp.where(side == 1, table[cell * 16 + tile + tiles - 1, source], lines)
                least = jnp.where(side == -1, table[64 + cell * 16 + tile, source], 0)
                span = jnp.maximum(most - least, 0)
                ox = [x - up.astype(F32) for x in place_x]
                oy = [y - side.astype(F32) for y in place_y]

                def some(b, weight):
                    weight = list(weight)
                    for r in range(4):
                        at, to = least + b * 4 + r, front + b * 4 + r
                        x = spots[source, 0, pl.ds(at, 1), :]
                        y = spots[source, 1, pl.ds(at, 1), :]
                        z = spots[source, 2, pl.ds(at, 1), :]
                        take = pl.ds(pl.multiple_of(q * 160 + at * 8, 8), 8)
                        queue[pl.ds(pl.multiple_of(to * 8, 8), 8), :] = sent[take, :]
                        for t in range(tiles):
                            dx, dy, dz = ox[t] - x, oy[t] - y, oz[t] - z
                            d = dx * dx + dy * dy + dz * dz
                            c = jnp.maximum(1.0 - d, 0.0)
                            c = c * c
                            put = pl.ds(pl.multiple_of(to * 16 + 8 * t, 8), 8)
                            far[put, :] = d
                            close[put, :] = c
                            weight[t] = weight[t] + c
                    return tuple(weight)

                weight = lax.fori_loop(0, (span + 3) >> 2, some, weight)
                return (front + span,) + tuple(weight)

            nothing = jnp.zeros((8, 128), F32)
            carry = lax.fori_loop(0, entries, measure, (jnp.int32(0),) + (nothing,) * tiles)
            front = carry[0]
            for t in range(tiles):
                csum[pl.ds(start + 8 * t, 8), :] = carry[1 + t]
            for r in range(3):
                queue[pl.ds(pl.multiple_of((front + r) * 8, 8), 8), :] = nothing
                for t in range(tiles):
                    far[pl.ds(pl.multiple_of((front + r) * 16 + 8 * t, 8), 8), :] = nothing
                    close[pl.ds(pl.multiple_of((front + r) * 16 + 8 * t, 8), 8), :] = nothing

            first = pl.multiple_of(start * 8, 64)
            nr = [floor[pl.ds(first + 8 * i, 8), :] for i in range(size)]

            def senders(b, carry):
                sums = list(carry)
                for r in range(4):
                    at = b * 4 + r
                    s = queue[pl.ds(pl.multiple_of(at * 8, 8), 8), :]
                    for i in range(size):
                        d = far[pl.ds(at * 16 + i, 1), :]
                        c = close[pl.ds(at * 16 + i, 1), :]
                        sums[i] = sums[i] + c * jnp.maximum(s + d * pull, nr[i])
                return tuple(sums)

            sums = lax.fori_loop(0, (front + 3) >> 2, senders, (nothing,) * size)
            for i in range(size):
                acc[pl.ds(first + 8 * i, 8), :] = sums[i]

        def pair_of_tiles(b, _):
            block_of(2, 2 * b)
            return 0

        def odd_tile(b, _):
            block_of(1, b)
            return 0

        tiles = (here + 7) >> 3
        lax.fori_loop(0, tiles >> 1, pair_of_tiles, 0)
        lax.fori_loop(tiles & ~1, tiles, odd_tile, 0)
        return 0

    lax.fori_loop(0, 4, one_cell, 0)

    for cell in range(4):

        def gather(group, _, cell=cell):
            lane = iota((8, 128), 1)
            for t in range(4):
                at = pl.multiple_of(group * 32 + 8 * t, 8)
                base = (cell * 128 + at) * 8
                parts = [acc[pl.ds(base + q, 8, stride=8), :] for q in range(8)]
                for bit in (4, 2, 1):
                    low = (lane & (16 * bit)) == 0
                    parts = [
                        jnp.where(low, parts[q], parts[q + bit])
                        + swap_lanes(jnp.where(low, parts[q + bit], parts[q]), 16 * bit)
                        for q in range(bit)
                    ]
                weight = jnp.sum(csum[pl.ds(cell * 128 + at, 8), :], axis=1, keepdims=True) * (1.0 / 16.0)
                incoming[pl.ds(cell * 128 + at, 8), :] = parts[0] + recv[cell, pl.ds(at, 8), :] * weight
            return 0

        lax.fori_loop(0, (counts[cell] + 31) >> 5, gather, 0)

    rounded = (incoming[...] * (8.0 / 128.0)).astype(BF16)
    if not last:
        msg_in[...] = rounded
        return
    new = node_update(step, state, rounded, w_self, w_msg, b_node, w_out, gain)
    slot = iota((128, 128), 0).astype(F32)
    for cell in range(4):
        given = (cell & 1) * 2 + (cell >> 1)
        perm = (slot == ranks[given : given + 1, :]).astype(F32).astype(BF16)
        here = new[cell * 128 : cell * 128 + 128]
        back = lax.dot_general(perm, here, (((0,), (0,)), ((), ())), preferred_element_type=F32)
        out[given] = back.astype(BF16)


def per_device(
    latent, offset, occupied, pair_list, w_send, w_recv, b_edge, w_disp, w_dist, w_self, w_msg, b_node, w_out, gain
):
    shape = jax.ShapeDtypeStruct
    w_disp = w_disp.transpose(1, 0, 2)
    sems = [pltpu.SemaphoreType.DMA((6,)), pltpu.SemaphoreType.DMA((6,)), pltpu.SemaphoreType.DMA]
    work = [pltpu.VMEM((4, ROWS, 128), BF16), pltpu.VMEM((512, 128), F32), pltpu.VMEM((512, 128), F32)]
    cells, wide = shape((4, 128, 128), BF16), shape((4, 128, 128), F32)
    state, ranks, recv, place, grid, table = pl.pallas_call(
        begin,
        name="begin",
        out_shape=(
            cells,
            shape((4, 128), F32),
            wide,
            shape((4, 3, 128, 128), F32),
            shape((12, ROWS, 128), BF16),
            shape((136, 128), jnp.int32),
        ),
        in_specs=[FIXED, VMEM, VMEM, FIXED, FIXED, VMEM, VMEM],
        out_specs=(VMEM,) * 6,
        scratch_shapes=work
        + sems
        + [pltpu.VMEM((4, 128, 128), BF16), pltpu.VMEM((2, 128, 128), BF16), pltpu.VMEM((2, 128, 128), BF16)]
        + [pltpu.SemaphoreType.DMA((3,))],
        compiler_params=pltpu.CompilerParams(collective_id=0, has_side_effects=True, vmem_limit_bytes=LIMIT),
    )(
        latent.reshape(4, 128, 128),
        offset.transpose(0, 2, 1, 3),
        occupied.reshape(4, 128),
        w_send,
        w_recv,
        b_edge,
        w_disp,
    )
    codes = pair_list.reshape(-1)
    scratch = [
        pltpu.VMEM((4096, 128), F32),
        pltpu.VMEM((4096, 128), F32),
        pltpu.VMEM((512, 128), F32),
        pltpu.VMEM((9 * 160, 128), F32),
        pltpu.VMEM((148 * 8, 128), F32),
        pltpu.VMEM((12, 3, 24, 128), F32),
        pltpu.VMEM((148 * 16, 128), F32),
        pltpu.VMEM((148 * 16, 128), F32),
        pltpu.VMEM((512, 128), F32),
        pltpu.SMEM((4, 27), jnp.int32),
        pltpu.SMEM((4,), jnp.int32),
    ]
    msg_in = pl.pallas_call(
        functools.partial(pairs, 0, False),
        name="pairs_0",
        out_shape=shape((512, 128), BF16),
        in_specs=[SMEM] * 2 + [VMEM] * 5,
        out_specs=VMEM,
        scratch_shapes=scratch,
        compiler_params=pltpu.CompilerParams(vmem_limit_bytes=LIMIT),
    )(codes, table, grid, recv, place, w_disp, w_dist)
    state, recv, grid = pl.pallas_call(
        middle,
        name="middle",
        out_shape=(cells, wide, shape((12, ROWS, 128), BF16)),
        in_specs=[VMEM] * 13,
        out_specs=(VMEM,) * 3,
        scratch_shapes=work + sems,
        compiler_params=pltpu.CompilerParams(collective_id=1, has_side_effects=True, vmem_limit_bytes=LIMIT),
    )(state, msg_in, grid, place, w_send, w_recv, b_edge, w_disp, w_self, w_msg, b_node, w_out, gain)
    out = pl.pallas_call(
        functools.partial(pairs, 1, True),
        name="pairs_1",
        out_shape=cells,
        in_specs=[SMEM] * 2 + [VMEM] * 12,
        out_specs=VMEM,
        scratch_shapes=scratch,
        compiler_params=pltpu.CompilerParams(vmem_limit_bytes=LIMIT),
    )(codes, table, grid, recv, place, w_disp, w_dist, state, ranks, w_self, w_msg, b_node, w_out, gain)
    return out.reshape(latent.shape)


def solution(mesh):
    return jax.shard_map(
        per_device,
        mesh=mesh,
        in_specs=(
            P("len", "wid", None, None),
            P("len", "wid", None, None),
            P("len", "wid", None),
            P("len", "wid", None),
        )
        + (P(),) * 10,
        out_specs=P("len", "wid", None, None),
        check_vma=False,
    )
```

time: 108 us -> 96.8 us (0.90)
  the two profiles are of different devices: /device:TPU:257 before, /device:TPU:1 now
where the time goes in v1:
time: 96.8 us; the launch traced here: 97.8 us
  Pallas kernels  93.6 us (97%)
  local copies, waits for them, and re-layouts  4 us (4%)
    pallas_call x1, Pallas kernels, per_device(): pl.pallas_call(functools.partial(pairs, 1, True), name='pairs_1', out_sha...  30.2 us
    pallas_call x1, Pallas kernels, per_device(): pl.pallas_call(functools.partial(pairs, 0, False), name='pairs_0', out_sh...  28.8 us
    pallas_call x1, Pallas kernels, per_device(): pl.pallas_call(begin, name='begin', out_shape=(cells, shape((4, 128), F32...  22 us
    pallas_call x1, Pallas kernels, per_device(): pl.pallas_call(middle, name='middle', out_shape=(cells, wide, shape((12,...  12.6 us
    unnamed x32, local copies, waits for them, and re-layouts  4 us

profile of v1, /device:TPU:1, one launch (start us, length us, event | category | flops | bytes accessed | tf_op | source)
XLA Modules:
  0.0 97.8 jit_solution(14094636289021886327)
XLA Ops:
  0.0 0.0 copy-start.9
  0.0 0.7 copy-done.14
  0.7 0.0 copy-done.13
  0.7 0.0 copy-done.8
  0.7 0.0 copy-done.9
  0.7 0.8 copy-done.3
  1.6 0.8 copy-done.5
  2.4 0.9 copy-done.7
  3.3 22.0 %begin.1 = (bf16[4,128,128]{2,1,0:T(8,128)(2,1)S(1)}, f32[4,128]{1,0:T(4,128)S(1)}, f32[4,128,128]{2,1,0:T(8,128)S(1)}, f32[4,3,128,128]{3,2,1,0:T(8,128)S(1)}, ...) custom-call(bf16[4,128,128]{2,1,0:T(8,128)(2,1)S(1)} %bitcast.6, bf16[2,3,2,128]{3,2,1,0:T(2,128)(2,1)S(1)} %bitcast.11, ...), custom_call_target="tpu_custom_call" | custom-call | tf_op jit(solution)/shard_map/begin/pallas_call | solution.py:451
  25.3 0.0 copy-start.10
  25.3 0.0 copy-start.15
  25.3 0.7 copy-done.10
  26.0 0.0 copy-done.15
  26.0 0.0 copy-start.4
  26.0 0.0 copy-start.6
  26.0 0.0 copy-start.11
  26.0 0.0 copy-start.12
  26.1 28.8 %pairs_0.1.msg_in = bf16[512,128]{1,0:T(8,128)(2,1)S(1)} custom-call(s32[36]{0:T(128)S(1)} %bitcast.13, s32[136,128]{1,0:T(8,128)S(1)} %get-tuple-element.14.table, bf16[12,144,128]{2,1,0:T(8,128)(2,1)S(1)} %get-tuple-element.16.grid.before, f32[4,128,128]{2,1,0:T(8,128)S(1)} %get-tuple-element.17.recv, f32[4,3,128,128]{3,2,1,0:T(8,128)S(1)} %get-tuple-element.18.place, ...), custom_call_target="tpu_custom_call" | custom-call | tf_op jit(solution)/shard_map/pairs_0/pallas_call | solution.py:492
  54.8 0.0 copy-done
  54.9 0.0 copy-done.1
  54.9 0.0 copy-done.2
  54.9 0.0 copy-done.4
  54.9 12.6 %middle.1 = (bf16[4,128,128]{2,1,0:T(8,128)(2,1)S(1)}, f32[4,128,128]{2,1,0:T(8,128)S(1)}, bf16[12,144,128]{2,1,0:T(8,128)(2,1)S(1)}) custom-call(bf16[4,128,128]{2,1,0:T(8,128)(2,1)S(1)} %get-tuple-element.15.state, bf16[512,128]{1,0:T(8,128)(2,1)S(1)} %pairs_0.1.msg_in, bf16[12,144,128]{2,1,0:T(8,128)(2,1)S(1)} %get-tuple-element.16.grid.before, ...), custom_call_target="tpu_custom_call" | custom-call | tf_op jit(solution)/shard_map/middle/pallas_call | solution.py:501
  67.5 30.2 %pairs_1.1 = bf16[4,128,128]{2,1,0:T(8,128)(2,1)} custom-call(s32[36]{0:T(128)S(1)} %bitcast.14, s32[136,128]{1,0:T(8,128)S(1)} %get-tuple-element.14.table, bf16[12,144,128]{2,1,0:T(8,128)(2,1)S(1)} %get-tuple-element.19.grid, f32[4,128,128]{2,1,0:T(8,128)S(1)} %get-tuple-element.20.recv, f32[4,3,128,128]{3,2,1,0:T(8,128)S(1)} %get-tuple-element.18.place, ...), custom_call_target="tpu_custom_call" | custom-call | tf_op jit(solution)/shard_map/pairs_1/pallas_call | solution.py:510
  (12 shorter events, 0.0 us)
Async XLA Ops:
  0.0 0.7 copy-start.14
  0.0 0.7 copy-start.13
  0.0 0.7 copy-start.8
  0.0 0.7 copy-start.9
  0.7 0.8 copy-start.3
  1.6 0.8 copy-start.5
  2.4 0.9 copy-start.7
  25.3 0.7 copy-start.10
  25.3 0.7 copy-start.15
  26.0 28.8 %copy-start = (bf16[2,128,128]{2,1,0:T(8,128)(2,1)S(1)}, bf16[2,128,128]{2,1,0:T(8,128)(2,1)}, u32[]{:S(2)}) copy-start(bf16[2,128,128]{2,1,0:T(8,128)(2,1)} %refs_2_.3) | copy-start | bytes 196612
  26.0 28.9 %copy-start.1 = (bf16[2,128,128]{2,1,0:T(8,128)(2,1)S(1)}, bf16[2,128,128]{2,1,0:T(8,128)(2,1)}, u32[]{:S(2)}) copy-start(bf16[2,128,128]{2,1,0:T(8,128)(2,1)} %refs_3_.3) | copy-start | bytes 196612
  26.0 28.9 %copy-start.2 = (bf16[2,128,128]{2,1,0:T(8,128)(2,1)S(1)}, bf16[2,128,128]{2,1,0:T(8,128)(2,1)}, u32[]{:S(2)}) copy-start(bf16[2,128,128]{2,1,0:T(8,128)(2,1)} %refs_5_.1) | copy-start | bytes 196612
  26.0 28.9 %copy-start.4 = (bf16[2,128,128]{2,1,0:T(8,128)(2,1)S(1)}, bf16[2,128,128]{2,1,0:T(8,128)(2,1)}, u32[]{:S(2)}) copy-start(bf16[2,128,128]{2,1,0:T(8,128)(2,1)} %w_send.1) | copy-start | bytes 196612
  26.0 28.9 %copy-start.6 = (bf16[2,128,128]{2,1,0:T(8,128)(2,1)S(1)}, bf16[2,128,128]{2,1,0:T(8,128)(2,1)}, u32[]{:S(2)}) copy-start(bf16[2,128,128]{2,1,0:T(8,128)(2,1)} %w_recv.1) | copy-start | bytes 196612
  26.0 28.9 %copy-start.11 = (f32[2,128]{1,0:T(2,128)S(1)}, f32[2,128]{1,0:T(2,128)}, u32[]{:S(2)}) copy-start(f32[2,128]{1,0:T(2,128)} %refs_4_.3) | copy-start | bytes 3076
  26.0 28.9 %copy-start.12 = (f32[2,128]{1,0:T(2,128)S(1)}, f32[2,128]{1,0:T(2,128)}, u32[]{:S(2)}) copy-start(f32[2,128]{1,0:T(2,128)} %refs_6_.1) | copy-start | bytes 3076
